TPU v7x, 32 devices: a whole 2x2x4 slice. The times are simulated.
32 devices in a mesh: seq: 8 (over z, x), dp: 4 (over y, core), grp: 1.
Axes of the slice: x: 2, y: 2, z: 4, core: 2. Of those that a mesh axis runs over, the one named last changes fastest.
Arguments:
- video_queries: bfloat16 [4, 1024, 4096], P('dp', 'seq', 'grp'), may hold values from -13.5 to 13.5
- caption_keys: bfloat16 [4, 512, 4096], P('dp', 'seq', 'grp'), may hold values from -6 to 6
- caption_values: bfloat16 [4, 512, 4096], P('dp', 'seq', 'grp'), may hold values from -6 to 6
- out_grad: bfloat16 [4, 1024, 4096], P('dp', 'seq', 'grp'), may hold values from -6 to 6
- head_gate: float32 [32], replicated, may hold values from 0.25 to 2
- video_len: int32 [4], P('dp'), may hold values from 1 to 1024, 2048 in all
- cap_len: int32 [4], P('dp'), may hold values from 1 to 512, 1024 in all
Outputs:
- attended: bfloat16 [4, 1024, 4096], P('dp', 'seq', 'grp')
- query_grad: bfloat16 [4, 1024, 4096], P('dp', 'seq', 'grp')
- key_grad: bfloat16 [4, 512, 4096], P('dp', 'seq', 'grp')
- value_grad: bfloat16 [4, 512, 4096], P('dp', 'seq', 'grp')
- gate_grad: float32 [32], replicated
All inputs are finite; a program needn't handle non-finite values. No bound on the sum of `video_len` or of `cap_len` on one device may be relied on, other than what follows from the above.
Results may differ from a plain program's by a relative error of at most 0.017.
Values may be sent and summed in bfloat16 or wider, within the bound.
A program may use at most 64 MiB of HBM per device.

v0:
```python
import jax
import jax.numpy as jnp
from jax import lax
from jax.sharding import PartitionSpec as P


def compute(query_blocks, cotangent, cap_keys, values, key_live, row_live, gates):
    blocks, row_count, columns = query_blocks.shape
    captions = cap_keys.shape[0]
    head_count = gates.shape[0]
    head_width = columns // head_count
    score_scale = head_width ** (-0.5)
    query_heads = query_blocks.reshape(blocks, row_count, head_count, head_width)
    key_heads = cap_keys.reshape(captions, head_count, head_width)
    value_heads = values.reshape(captions, head_count, head_width)
    scores = (
        jnp.einsum("bthd,jhd->bhtj", query_heads, key_heads, preferred_element_type=jnp.float32)
        * score_scale
    )
    scores = jnp.where(key_live[None, None, None, :], scores, -jnp.inf)
    shifted = jnp.exp(scores - jnp.max(scores, axis=-1, keepdims=True))
    weights = shifted / jnp.sum(shifted, axis=-1, keepdims=True)
    weights_low = weights.astype(jnp.bfloat16)
    attention = jnp.einsum(
        "bhtj,jhd->bthd", weights_low, value_heads, preferred_element_type=jnp.float32
    )
    live_rows = row_live[:, :, None, None]
    head_scale = gates[None, None, :, None]
    attended = (
        (attention * head_scale * live_rows)
        .astype(jnp.bfloat16)
        .reshape(blocks * row_count, columns)
    )
    cot_heads = cotangent.reshape(blocks, row_count, head_count, head_width).astype(jnp.float32)
    gate_term = jnp.sum(cot_heads * attention * live_rows, axis=(0, 1, 3))
    grad_attention = (cot_heads * head_scale * live_rows).astype(jnp.bfloat16)
    grad_weights = jnp.einsum(
        "bthd,jhd->bhtj", grad_attention, value_heads, preferred_element_type=jnp.float32
    )
    row_delta = jnp.sum(weights * grad_weights, axis=-1, keepdims=True)
    grad_scores = (weights * (grad_weights - row_delta) * score_scale).astype(jnp.bfloat16)
    query_grad = jnp.einsum(
        "bhtj,jhd->bthd", grad_scores, key_heads, preferred_element_type=jnp.float32
    )
    query_grad = query_grad.astype(jnp.bfloat16).reshape(blocks * row_count, columns)
    key_blocks = jnp.einsum(
        "bhtj,bthd->bjhd", grad_scores, query_heads, preferred_element_type=jnp.float32
    )
    value_blocks = jnp.einsum(
        "bhtj,bthd->bjhd", weights_low, grad_attention, preferred_element_type=jnp.float32
    )
    key_blocks = lax.optimization_barrier(key_blocks.astype(jnp.bfloat16)).astype(jnp.float32)
    value_blocks = lax.optimization_barrier(value_blocks.astype(jnp.bfloat16)).astype(jnp.float32)
    key_part = jnp.sum(key_blocks, axis=0).reshape(captions, columns)
    value_part = jnp.sum(value_blocks, axis=0).reshape(captions, columns)
    return (attended, query_grad, key_part, value_part, gate_term)


def per_device(
    video_queries, caption_keys, caption_values, out_grad, head_gate, video_len, cap_len
):
    row_count = video_queries.shape[1]
    local_width = video_queries.shape[2]
    head_count = head_gate.shape[0]
    seq_count = lax.axis_size("seq")
    grp_count = lax.axis_size("grp")
    seq_index = lax.axis_index("seq")
    grp_index = lax.axis_index("grp")
    local_heads = head_count // grp_count
    head_start = grp_index * local_heads
    columns = local_width // seq_count
    group_heads = local_heads // seq_count
    mine_queries, mine_cot = (
        lax.all_to_all(video_queries[0], "seq", split_axis=1, concat_axis=0, tiled=True),
        lax.all_to_all(out_grad[0], "seq", split_axis=1, concat_axis=0, tiled=True),
    )
    keys_all, values_all = (
        lax.all_to_all(caption_keys[0], "seq", split_axis=1, concat_axis=0, tiled=True),
        lax.all_to_all(caption_values[0], "seq", split_axis=1, concat_axis=0, tiled=True),
    )
    captions = keys_all.shape[0]
    row_index = (
        jnp.arange(seq_count, dtype=jnp.int32)[:, None] * row_count
        + jnp.arange(row_count, dtype=jnp.int32)[None, :]
    )
    row_live = (row_index < video_len[0]).astype(jnp.float32)
    key_live = jnp.arange(captions, dtype=jnp.int32) < cap_len[0]
    gate_start = head_start + seq_index * group_heads
    gates = lax.dynamic_slice_in_dim(head_gate, gate_start, group_heads)
    query_blocks = mine_queries.reshape(seq_count, row_count, columns)
    cot_blocks = mine_cot.reshape(seq_count, row_count, columns)
    results = compute(query_blocks, cot_blocks, keys_all, values_all, key_live, row_live, gates)
    attended, query_grad, key_part, value_part, gate_term = results
    attended_rows, query_rows = (
        lax.all_to_all(attended, "seq", split_axis=0, concat_axis=1, tiled=True),
        lax.all_to_all(query_grad, "seq", split_axis=0, concat_axis=1, tiled=True),
    )
    key_rows, value_rows = (
        lax.all_to_all(
            key_part.astype(jnp.bfloat16), "seq", split_axis=0, concat_axis=1, tiled=True
        ),
        lax.all_to_all(
            value_part.astype(jnp.bfloat16), "seq", split_axis=0, concat_axis=1, tiled=True
        ),
    )
    gate_full = lax.dynamic_update_slice(
        jnp.zeros((head_count,), jnp.float32), gate_term, (gate_start,)
    )
    outputs = (attended_rows[None], query_rows[None], key_rows[None], value_rows[None])
    gate_grad = lax.psum(gate_full, ("seq", "dp", "grp"))
    return (outputs[0], outputs[1], outputs[2], outputs[3], gate_grad)


def solution(mesh):
    in_specs = (
        P("dp", "seq", "grp"),
        P("dp", "seq", "grp"),
        P("dp", "seq", "grp"),
        P("dp", "seq", "grp"),
        P(),
        P("dp"),
        P("dp"),
    )
    out_specs = (
        P("dp", "seq", "grp"),
        P("dp", "seq", "grp"),
        P("dp", "seq", "grp"),
        P("dp", "seq", "grp"),
        P(),
    )
    return jax.shard_map(
        per_device, mesh=mesh, in_specs=in_specs, out_specs=out_specs, check_vma=False
    )
```

profile of v0, /device:TPU:0, one launch (start us, length us, event | category | flops | bytes accessed | tf_op | source)
XLA Modules:
  0.0 249.1 jit_solution(871145652880503635)
XLA Ops:
  2.9 7.3 %all-to-all-start = ((bf16[64,8,512]{2,0,1:T(8,128)(2,1)}), bf16[64,8,512]{2,0,1:T(8,128)(2,1)S(1)}, u32[]{:S(2)}, u32[]{:S(2)}) async-start(bf16[64,8,512]{2,0,1:T(8,128)(2,1)} %copy.71), calls=%async_computation | async-start | bytes 1048576 | tf_op jit(solution)/shard_map/all_to_all | solution.py:78
  12.4 12.3 %all-to-all-done = bf16[64,8,512]{2,0,1:T(8,128)(2,1)S(1)} async-done(((bf16[64,8,512]{2,0,1:T(8,128)(2,1)}), bf16[64,8,512]{2,0,1:T(8,128)(2,1)S(1)}, u32[]{:S(2)}, u32[]{:S(2)}) %all-to-all-start) | async-done | bytes 524320 | tf_op jit(solution)/shard_map/all_to_all | solution.py:78
  24.7 3.6 %all-to-all-start.2 = ((bf16[64,8,512]{2,0,1:T(8,128)(2,1)}), bf16[64,8,512]{2,0,1:T(8,128)(2,1)S(1)}, u32[]{:S(2)}, u32[]{:S(2)}) async-start(bf16[64,8,512]{2,0,1:T(8,128)(2,1)} %copy.75), calls=%async_computation.2 | async-start | bytes 1048576 | tf_op jit(solution)/shard_map/all_to_all | solution.py:79
  30.6 12.4 %all-to-all-done.2 = bf16[64,8,512]{2,0,1:T(8,128)(2,1)S(1)} async-done(((bf16[64,8,512]{2,0,1:T(8,128)(2,1)}), bf16[64,8,512]{2,0,1:T(8,128)(2,1)S(1)}, u32[]{:S(2)}, u32[]{:S(2)}) %all-to-all-start.2) | async-done | bytes 524320 | tf_op jit(solution)/shard_map/all_to_all | solution.py:79
  43.0 3.6 %all-to-all-start.1 = ((bf16[128,8,512]{0,2,1:T(8,128)(2,1)}), bf16[128,8,512]{0,2,1:T(8,128)(2,1)S(1)}, u32[]{:S(2)}, u32[]{:S(2)}) async-start(bf16[128,8,512]{0,2,1:T(8,128)(2,1)} %bitcast.3), calls=%async_computation.1 | async-start | bytes 2097152 | tf_op jit(solution)/shard_map/all_to_all | solution.py:74
  50.0 22.6 %all-to-all-done.1 = bf16[128,8,512]{0,2,1:T(8,128)(2,1)S(1)} async-done(((bf16[128,8,512]{0,2,1:T(8,128)(2,1)}), bf16[128,8,512]{0,2,1:T(8,128)(2,1)S(1)}, u32[]{:S(2)}, u32[]{:S(2)}) %all-to-all-start.1) | async-done | bytes 1048608 | tf_op jit(solution)/shard_map/all_to_all | solution.py:74
  72.6 3.7 %all-to-all-start.4 = ((bf16[128,8,512]{0,2,1:T(8,128)(2,1)}), bf16[128,8,512]{0,2,1:T(8,128)(2,1)S(1)}, u32[]{:S(2)}, u32[]{:S(2)}) async-start(bf16[128,8,512]{0,2,1:T(8,128)(2,1)} %bitcast.86), calls=%async_computation.4 | async-start | bytes 2097152 | tf_op jit(solution)/shard_map/all_to_all | solution.py:75
  77.6 3.9 %fusion.44 = (f32[8,4,128]{2,0,1:T(8,128)S(1)}, f32[8,4,128,512]{2,3,0,1:T(8,128)S(1)}) fusion(f32[4,512,8,128]{3,1,2,0:T(8,128)S(1)} %fusion.26, pred[512]{0:T(512)(128)(4,1)S(1)} %iota_compare_fusion), kind=kOutput, calls=%fused_computation.48 | output fusion | flops 12583423 | bytes 16794112 | tf_op jit(solution)/shard_map/sub | solution.py:21
  81.5 3.2 %copy-done = f32[8,4,128,512]{2,3,0,1:T(8,128)} copy-done((f32[8,4,128,512]{2,3,0,1:T(8,128)}, f32[8,4,128,512]{2,3,0,1:T(8,128)S(1)}, u32[]{:S(2)}) %copy-start) | copy-done | bytes 8388632
  84.7 3.0 %fusion.43 = bf16[8,4,128,512]{2,3,0,1:T(8,128)(2,1)} fusion(f32[8,4,128,512]{2,3,0,1:T(8,128)S(1)} %get-tuple-element.24, f32[8,4,128]{2,0,1:T(8,128)S(1)} %get-tuple-element.23), kind=kLoop, calls=%fused_computation.47 | loop fusion | flops 4194304 | bytes 12599296 | tf_op jit(solution)/shard_map/convert_element_type | solution.py:23
  87.7 14.5 %all-to-all-done.4 = bf16[128,8,512]{0,2,1:T(8,128)(2,1)S(1)} async-done(((bf16[128,8,512]{0,2,1:T(8,128)(2,1)}), bf16[128,8,512]{0,2,1:T(8,128)(2,1)S(1)}, u32[]{:S(2)}, u32[]{:S(2)}) %all-to-all-start.4) | async-done | bytes 1048608 | tf_op jit(solution)/shard_map/all_to_all | solution.py:75
  102.3 4.3 %fusion.24 = (f32[4]{0:T(128)S(1)}, bf16[8,128,4,128]{1,3,0,2:T(8,128)(2,1)S(1)}, bf16[8,128,4,128]{1,3,0,2:T(8,128)(2,1)}) fusion(f32[8,128,4,128]{1,3,2,0:T(8,128)S(1)} %bitcast.83, f32[8,128]{1,0:T(8,128)S(1)} %fusion.40, f32[4]{0:T(128)S(1)} %dynamic_slice.3, bf16[8,4,128,512]{2,3,0,1:T(8,128)(2,1)} %fusion.43, bf16[512,4,128,1]{2,1,0,3:T(4,128)(2,1)S(1)} %bitcast.89), kind=kOutput, calls=%fused_computation.28 | convolution fusion | flops 541589504 | bytes 8917024 | tf_op jit(solution)/shard_map/bhtj,jhd->bthd/dot_general | solution.py:24
  106.6 9.8 %fusion.4 = bf16[8,4,128,512]{2,3,0,1:T(8,128)(2,1)} fusion(bf16[8,128,4,128]{1,3,0,2:T(8,128)(2,1)S(1)} %get-tuple-element.21, bf16[512,4,128,1]{2,1,0,3:T(4,128)(2,1)S(1)} %bitcast.90, f32[8,4,128,512]{2,3,0,1:T(8,128)} %copy-done, f32[8,4,128]{2,0,1:T(8,128)S(1)} %get-tuple-element.23), kind=kOutput, calls=%fused_computation.6 | convolution fusion | flops 1088426496 | bytes 14172160 | tf_op jit(solution)/shard_map/sub | solution.py:41
  116.4 5.4 %convert_bitcast_fusion.1 = bf16[8,512,4,128]{3,1,2,0:T(8,128)(2,1)} fusion(bf16[8,128,4,128]{1,3,2,0:T(8,128)(2,1)S(1)} %bitcast.85, bf16[8,4,128,512]{2,3,0,1:T(8,128)(2,1)} %fusion.4), kind=kOutput, calls=%fused_computation.17 | convolution fusion | flops 538968064 | bytes 9437184 | tf_op jit(solution)/shard_map/bhtj,bthd->bjhd/dot_general | solution.py:46
  126.0 3.7 %all-to-all-start.6 = ((bf16[8,64,512]{2,1,0:T(8,128)(2,1)}), bf16[8,64,512]{2,1,0:T(8,128)(2,1)S(1)}, u32[]{:S(2)}, u32[]{:S(2)}) async-start(bf16[8,64,512]{2,1,0:T(8,128)(2,1)} %convert_element_type.70), calls=%async_computation.6 | async-start | bytes 1048576 | tf_op jit(solution)/shard_map/all_to_all | solution.py:99
  129.8 5.4 %convert_bitcast_fusion = bf16[8,512,4,128]{1,3,2,0:T(8,128)(2,1)} fusion(bf16[8,4,128,512]{2,3,0,1:T(8,128)(2,1)} %fusion.43, bf16[8,128,4,128]{1,3,0,2:T(8,128)(2,1)S(1)} %get-tuple-element.21), kind=kOutput, calls=%fused_computation.16 | convolution fusion | flops 538968064 | bytes 9437184 | tf_op jit(solution)/shard_map/bhtj,bthd->bjhd/dot_general | solution.py:49
  139.3 5.0 %all-to-all-done.6 = bf16[8,64,512]{2,1,0:T(8,128)(2,1)S(1)} async-done(((bf16[8,64,512]{2,1,0:T(8,128)(2,1)}), bf16[8,64,512]{2,1,0:T(8,128)(2,1)S(1)}, u32[]{:S(2)}, u32[]{:S(2)}) %all-to-all-start.6) | async-done | bytes 524320 | tf_op jit(solution)/shard_map/all_to_all | solution.py:99
  144.3 3.6 %all-to-all-start.7 = ((bf16[8,64,512]{2,1,0:T(8,128)(2,1)}), bf16[8,64,512]{2,1,0:T(8,128)(2,1)S(1)}, u32[]{:S(2)}, u32[]{:S(2)}) async-start(bf16[8,64,512]{2,1,0:T(8,128)(2,1)} %convert_element_type.73), calls=%async_computation.7 | async-start | bytes 1048576 | tf_op jit(solution)/shard_map/all_to_all | solution.py:102
  148.0 2.9 %fusion.25 = bf16[8,128,4,128]{1,3,0,2:T(8,128)(2,1)S(1)} fusion(bf16[512,4,128,1]{0,2,3,1:T(8,128)(2,1)S(1)} %copy.106, bf16[8,4,128,512]{2,3,0,1:T(8,128)(2,1)} %fusion.4), kind=kOutput, calls=%fused_computation.31 | convolution fusion | flops 537395200 | bytes 5767168 | tf_op jit(solution)/shard_map/bhtj,jhd->bthd/dot_general | solution.py:42
  152.0 10.7 %all-to-all-done.7 = bf16[8,64,512]{2,1,0:T(8,128)(2,1)S(1)} async-done(((bf16[8,64,512]{2,1,0:T(8,128)(2,1)}), bf16[8,64,512]{2,1,0:T(8,128)(2,1)S(1)}, u32[]{:S(2)}, u32[]{:S(2)}) %all-to-all-start.7) | async-done | bytes 524320 | tf_op jit(solution)/shard_map/all_to_all | solution.py:102
  162.6 3.6 %all-to-all-start.5 = ((bf16[8,128,512]{1,2,0:T(8,128)(2,1)}), bf16[8,128,512]{1,2,0:T(8,128)(2,1)S(1)}, u32[]{:S(2)}, u32[]{:S(2)}) async-start(bf16[8,128,512]{1,2,0:T(8,128)(2,1)} %bitcast.21), calls=%async_computation.5 | async-start | bytes 2097152 | tf_op jit(solution)/shard_map/all_to_all | solution.py:96
  167.3 24.9 %all-to-all-done.5 = bf16[8,128,512]{1,2,0:T(8,128)(2,1)S(1)} async-done(((bf16[8,128,512]{1,2,0:T(8,128)(2,1)}), bf16[8,128,512]{1,2,0:T(8,128)(2,1)S(1)}, u32[]{:S(2)}, u32[]{:S(2)}) %all-to-all-start.5) | async-done | bytes 1048608 | tf_op jit(solution)/shard_map/all_to_all | solution.py:96
  192.2 3.6 %all-to-all-start.3 = ((bf16[8,128,512]{1,2,0:T(8,128)(2,1)}), bf16[8,128,512]{1,2,0:T(8,128)(2,1)S(1)}, u32[]{:S(2)}, u32[]{:S(2)}) async-start(bf16[8,128,512]{1,2,0:T(8,128)(2,1)} %bitcast.11), calls=%async_computation.3 | async-start | bytes 2097152 | tf_op jit(solution)/shard_map/all_to_all | solution.py:95
  196.1 45.9 %psum.7 = f32[32]{0:T(128)} all-reduce(f32[32]{0:T(128)S(1)} %dynamic_update_slice.3), channel_id=1, replica_groups=mesh['seq'=8,'dp'=4,'grp'=1] {'seq','dp','grp'}, use_global_device_ids=true, to_apply=%region_6.7 | all-reduce | flops 32 | bytes 256 | tf_op jit(solution)/shard_map/psum | solution.py:110
  (39 shorter events, 28.0 us)
Async XLA Ops:
  0.6 46.6 %copy-start.2 = (bf16[1,128,4096]{2,1,0:T(8,128)(2,1)S(1)}, bf16[1,128,4096]{2,1,0:T(8,128)(2,1)}, u32[]{:S(2)}) copy-start(bf16[1,128,4096]{2,1,0:T(8,128)(2,1)} %param.10) | copy-start | bytes 3145732
  0.6 48.6 %copy-start.3 = (f32[32]{0:T(128)S(1)}, f32[32]{0:T(128)}, u32[]{:S(2)}) copy-start(f32[32]{0:T(128)} %param.11) | copy-start | bytes 388
  2.9 21.8 %all-to-all-start = ((bf16[64,8,512]{2,0,1:T(8,128)(2,1)}), bf16[64,8,512]{2,0,1:T(8,128)(2,1)S(1)}, u32[]{:S(2)}, u32[]{:S(2)}) async-start(bf16[64,8,512]{2,0,1:T(8,128)(2,1)} %copy.71), calls=%async_computation | async-start | bytes 1048576 | tf_op jit(solution)/shard_map/all_to_all | solution.py:78
  24.7 18.3 %all-to-all-start.2 = ((bf16[64,8,512]{2,0,1:T(8,128)(2,1)}), bf16[64,8,512]{2,0,1:T(8,128)(2,1)S(1)}, u32[]{:S(2)}, u32[]{:S(2)}) async-start(bf16[64,8,512]{2,0,1:T(8,128)(2,1)} %copy.75), calls=%async_computation.2 | async-start | bytes 1048576 | tf_op jit(solution)/shard_map/all_to_all | solution.py:79
  43.0 29.6 %all-to-all-start.1 = ((bf16[128,8,512]{0,2,1:T(8,128)(2,1)}), bf16[128,8,512]{0,2,1:T(8,128)(2,1)S(1)}, u32[]{:S(2)}, u32[]{:S(2)}) async-start(bf16[128,8,512]{0,2,1:T(8,128)(2,1)} %bitcast.3), calls=%async_computation.1 | async-start | bytes 2097152 | tf_op jit(solution)/shard_map/all_to_all | solution.py:74
  72.6 29.6 %all-to-all-start.4 = ((bf16[128,8,512]{0,2,1:T(8,128)(2,1)}), bf16[128,8,512]{0,2,1:T(8,128)(2,1)S(1)}, u32[]{:S(2)}, u32[]{:S(2)}) async-start(bf16[128,8,512]{0,2,1:T(8,128)(2,1)} %bitcast.86), calls=%async_computation.4 | async-start | bytes 2097152 | tf_op jit(solution)/shard_map/all_to_all | solution.py:75
  81.5 3.2 %copy-start = (f32[8,4,128,512]{2,3,0,1:T(8,128)}, f32[8,4,128,512]{2,3,0,1:T(8,128)S(1)}, u32[]{:S(2)}) copy-start(f32[8,4,128,512]{2,3,0,1:T(8,128)S(1)} %get-tuple-element.24) | copy-start | bytes 25165828
  126.0 18.3 %all-to-all-start.6 = ((bf16[8,64,512]{2,1,0:T(8,128)(2,1)}), bf16[8,64,512]{2,1,0:T(8,128)(2,1)S(1)}, u32[]{:S(2)}, u32[]{:S(2)}) async-start(bf16[8,64,512]{2,1,0:T(8,128)(2,1)} %convert_element_type.70), calls=%async_computation.6 | async-start | bytes 1048576 | tf_op jit(solution)/shard_map/all_to_all | solution.py:99
  138.0 28.3 %copy-start.1 = (bf16[8,128,4,128]{1,3,0,2:T(8,128)(2,1)S(1)}, bf16[8,128,4,128]{1,3,0,2:T(8,128)(2,1)}, u32[]{:S(2)}) copy-start(bf16[8,128,4,128]{1,3,0,2:T(8,128)(2,1)} %get-tuple-element.22) | copy-start | bytes 3145732
  144.3 18.3 %all-to-all-start.7 = ((bf16[8,64,512]{2,1,0:T(8,128)(2,1)}), bf16[8,64,512]{2,1,0:T(8,128)(2,1)S(1)}, u32[]{:S(2)}, u32[]{:S(2)}) async-start(bf16[8,64,512]{2,1,0:T(8,128)(2,1)} %convert_element_type.73), calls=%async_computation.7 | async-start | bytes 1048576 | tf_op jit(solution)/shard_map/all_to_all | solution.py:102
  162.6 29.6 %all-to-all-start.5 = ((bf16[8,128,512]{1,2,0:T(8,128)(2,1)}), bf16[8,128,512]{1,2,0:T(8,128)(2,1)S(1)}, u32[]{:S(2)}, u32[]{:S(2)}) async-start(bf16[8,128,512]{1,2,0:T(8,128)(2,1)} %bitcast.21), calls=%async_computation.5 | async-start | bytes 2097152 | tf_op jit(solution)/shard_map/all_to_all | solution.py:96
  192.2 55.6 %all-to-all-start.3 = ((bf16[8,128,512]{1,2,0:T(8,128)(2,1)}), bf16[8,128,512]{1,2,0:T(8,128)(2,1)S(1)}, u32[]{:S(2)}, u32[]{:S(2)}) async-start(bf16[8,128,512]{1,2,0:T(8,128)(2,1)} %bitcast.11), calls=%async_computation.3 | async-start | bytes 2097152 | tf_op jit(solution)/shard_map/all_to_all | solution.py:95
where the time goes:
time: 250 us; the launch traced here: 249 us
  waiting for transfers between devices  102 us (41%)
  blocking collectives  45.9 us (18%)
  starting transfers between devices  32.9 us (13%)
  matrix products  29.1 us (12%)
  local copies, waits for them, and re-layouts  24 us (10%)
  other arithmetic  12.8 us (5%)
    psum x1, blocking collectives, per_device(): gate_grad = lax.psum(gate_full, ('seq', 'dp', 'grp'))  45.9 us
    all_to_all x1, waiting for transfers between devices, per_device(): lax.all_to_all(query_grad, 'seq', split_axis=0, concat_axis=1, tiled=True)  24.9 us
    all_to_all x1, waiting for transfers between devices, per_device(): lax.all_to_all(video_queries[0], 'seq', split_axis=1, concat_axis=0, tile...  22.6 us
    all_to_all x1, waiting for transfers between devices, per_device(): lax.all_to_all(out_grad[0], 'seq', split_axis=1, concat_axis=0, tiled=True)  14.5 us
    all_to_all x1, waiting for transfers between devices, per_device(): lax.all_to_all(caption_values[0], 'seq', split_axis=1, concat_axis=0, til...  12.4 us
    all_to_all x1, waiting for transfers between devices, per_device(): lax.all_to_all(caption_keys[0], 'seq', split_axis=1, concat_axis=0, tiled...  12.3 us
    unnamed x14, local copies, waits for them, and re-layouts  11.9 us
    all_to_all x1, waiting for transfers between devices, per_device(): lax.all_to_all(value_part.astype(jnp.bfloat16), 'seq', split_axis=0, conc...  10.7 us
  transfers between devices with their start and end apart: 8, of which 7 were waited for; matrix products, arithmetic and copies ran while one was open for 14% of the time, Pallas kernels for 0%

commit v1 on v0

--- a/solution.py
+++ b/solution.py
@@ -2,6 +2,28 @@
 import jax.numpy as jnp
 from jax import lax
 from jax.sharding import PartitionSpec as P
+
+
+def in_blocks(x, dim, size):
+    before, after = (x.shape[:dim], x.shape[dim + 1 :])
+    return jnp.moveaxis(x.reshape(*before, size, -1, *after), dim, 0)
+
+
+def in_order(parts, dim):
+    shape = list(parts.shape[1:])
+    shape[dim] *= parts.shape[0]
+    return jnp.moveaxis(parts, 0, dim).reshape(shape)
+
+
+def exchange_in_pairs(array, axis, split_dim, concat_dim):
+    count, place = (lax.axis_size(axis), lax.axis_index(axis))
+    blocks = in_blocks(array, split_dim, count)
+    outs = [blocks[place]]
+    for step in range(1, count):
+        sent = blocks[place ^ step]
+        outs.append(lax.ppermute(sent, axis, [(i, i ^ step) for i in range(count)]))
+    blocks = jnp.stack(outs)[place ^ jnp.arange(count)]
+    return in_order(blocks, concat_dim)
 
 
 def compute(query_blocks, cotangent, cap_keys, values, key_live, row_live, gates):
@@ -76,7 +98,7 @@
     )
     keys_all, values_all = (
         lax.all_to_all(caption_keys[0], "seq", split_axis=1, concat_axis=0, tiled=True),
-        lax.all_to_all(caption_values[0], "seq", split_axis=1, concat_axis=0, tiled=True),
+        exchange_in_pairs(caption_values[0], "seq", 1, 0),
     )
     captions = keys_all.shape[0]
     row_index = (

time: 250 us -> 235 us (0.940)
  waiting for transfers between devices: 102 us -> 64.2 us
  starting transfers between devices: 32.9 us -> 46.7 us
  local copies, waits for them, and re-layouts: 24 us -> 33.7 us
    all_to_all x1, waiting for transfers between devices: 22.6 us -> 4.17 us  [per_device(): lax.all_to_all(video_queries[0], 'seq', split_axis=1, concat_axis=0, tile...]
    ppermute x0 -> x7, starting transfers between devices: none -> 13.2 us  [exchange_in_pairs(): outs.append(lax.ppermute(sent, axis, [(i, i ^ step) for i in range(count)]))]
    all_to_all x1 -> x0, waiting for transfers between devices: 12.4 us -> none  [per_device(): lax.all_to_all(caption_values[0], 'seq', split_axis=1, concat_axis=0, til...]
    all_to_all x1, waiting for transfers between devices: 10.7 us -> 0.01 us  [per_device(): lax.all_to_all(value_part.astype(jnp.bfloat16), 'seq', split_axis=0, conc...]
    ppermute x0 -> x7, waiting for transfers between devices: none -> 9.95 us  [exchange_in_pairs(): outs.append(lax.ppermute(sent, axis, [(i, i ^ step) for i in range(count)]))]
    all_to_all x1, waiting for transfers between devices: 12.3 us -> 3.26 us  [per_device(): lax.all_to_all(caption_keys[0], 'seq', split_axis=1, concat_axis=0, tiled...]
    unnamed x14 -> x30, local copies, waits for them, and re-layouts: 11.9 us -> 18.8 us
    all_to_all x1, waiting for transfers between devices: 4.99 us -> 9.45 us  [per_device(): lax.all_to_all(key_part.astype(jnp.bfloat16), 'seq', split_axis=0, concat...]
  transfers between devices with their start and end apart: 8 -> 14, of which waited for: 7 -> 7; matrix products, arithmetic and copies ran while one was open for 14% -> 22% of each run, Pallas kernels for 0% -> 0%
where the time goes in v1:
time: 235 us; the launch traced here: 233 us
  waiting for transfers between devices  64.2 us (27%)
  starting transfers between devices  46.7 us (20%)
  blocking collectives  45.7 us (19%)
  local copies, waits for them, and re-layouts  33.7 us (14%)
  matrix products  27.2 us (12%)
  other arithmetic  13.7 us (6%)
    psum x1, blocking collectives, per_device(): gate_grad = lax.psum(gate_full, ('seq', 'dp', 'grp'))  45.7 us
    all_to_all x1, waiting for transfers between devices, per_device(): lax.all_to_all(query_grad, 'seq', split_axis=0, concat_axis=1, tiled=True)  24.2 us
    unnamed x30, local copies, waits for them, and re-layouts  18.8 us
    ppermute x7, starting transfers between devices, exchange_in_pairs(): outs.append(lax.ppermute(sent, axis, [(i, i ^ step) for i in range(count)]))  13.2 us
    all_to_all x1, waiting for transfers between devices, per_device(): lax.all_to_all(out_grad[0], 'seq', split_axis=1, concat_axis=0, tiled=True)  13.2 us
    ppermute x7, waiting for transfers between devices, exchange_in_pairs(): outs.append(lax.ppermute(sent, axis, [(i, i ^ step) for i in range(count)]))  9.95 us
    sub x1, matrix products, compute(): grad_weights - row_delta  9.91 us
    all_to_all x1, waiting for transfers between devices, per_device(): lax.all_to_all(key_part.astype(jnp.bfloat16), 'seq', split_axis=0, concat...  9.45 us
  transfers between devices with their start and end apart: 14, of which 7 were waited for; matrix products, arithmetic and copies ran while one was open for 22% of the time, Pallas kernels for 0%

profile of v1, /device:TPU:0, one launch (start us, length us, event | category | flops | bytes accessed | tf_op | source)
XLA Modules:
  0.0 233.4 jit_solution(7313652531205831764)
XLA Ops:
  2.9 7.3 %all-to-all-start = ((bf16[64,8,512]{2,0,1:T(8,128)(2,1)}), bf16[64,8,512]{2,0,1:T(8,128)(2,1)S(1)}, u32[]{:S(2)}, u32[]{:S(2)}) async-start(bf16[64,8,512]{2,0,1:T(8,128)(2,1)} %copy.65), calls=%async_computation | async-start | bytes 1048576 | tf_op jit(solution)/shard_map/all_to_all | solution.py:100
  18.1 3.0 %collective-permute-start.3 = (bf16[64,512]{1,0:T(8,128)(2,1)S(1)}, bf16[64,512]{1,0:T(8,128)(2,1)}, u32[]{:S(2)}, u32[]{:S(2)}) collective-permute-start(bf16[64,512]{1,0:T(8,128)(2,1)S(1)} %bitcast.137), channel_id=1, source_target_pairs={{0,16},{4,20},{8,24},{12,28},{16,0},{20,4},{24,8},{28,12},{1,17},{... | collective-permute-start | bytes 196616 | tf_op jit(solution)/shard_map/ppermute | solution.py:24
  25.6 3.3 %all-to-all-done = bf16[64,8,512]{2,0,1:T(8,128)(2,1)S(1)} async-done(((bf16[64,8,512]{2,0,1:T(8,128)(2,1)}), bf16[64,8,512]{2,0,1:T(8,128)(2,1)S(1)}, u32[]{:S(2)}, u32[]{:S(2)}) %all-to-all-start) | async-done | bytes 524320 | tf_op jit(solution)/shard_map/all_to_all | solution.py:100
  28.9 3.6 %all-to-all-start.1 = ((bf16[128,8,512]{0,2,1:T(8,128)(2,1)}), bf16[128,8,512]{0,2,1:T(8,128)(2,1)S(1)}, u32[]{:S(2)}, u32[]{:S(2)}) async-start(bf16[128,8,512]{0,2,1:T(8,128)(2,1)} %bitcast.12), calls=%async_computation.1 | async-start | bytes 2097152 | tf_op jit(solution)/shard_map/all_to_all | solution.py:96
  35.2 3.8 %collective-permute-start.5 = (bf16[64,512]{1,0:T(8,128)(2,1)}, bf16[64,512]{1,0:T(8,128)(2,1)S(1)}, u32[]{:S(2)}, u32[]{:S(2)}) collective-permute-start(bf16[64,512]{1,0:T(8,128)(2,1)} %bitcast.139), channel_id=1, source_target_pairs={{0,24},{4,28},{8,16},{12,20},{16,8},{20,12},{24,0},{28,4},{1,25},{... | collective-permute-start | bytes 196616 | tf_op jit(solution)/shard_map/ppermute | solution.py:24
  44.7 8.5 %collective-permute-done.5 = bf16[64,512]{1,0:T(8,128)(2,1)S(1)} collective-permute-done((bf16[64,512]{1,0:T(8,128)(2,1)}, bf16[64,512]{1,0:T(8,128)(2,1)S(1)}, u32[]{:S(2)}, u32[]{:S(2)}) %collective-permute-start.5) | collective-permute-done | bytes 65568 | tf_op jit(solution)/shard_map/ppermute | solution.py:24
  55.8 4.2 %all-to-all-done.1 = bf16[128,8,512]{0,2,1:T(8,128)(2,1)S(1)} async-done(((bf16[128,8,512]{0,2,1:T(8,128)(2,1)}), bf16[128,8,512]{0,2,1:T(8,128)(2,1)S(1)}, u32[]{:S(2)}, u32[]{:S(2)}) %all-to-all-start.1) | async-done | bytes 1048608 | tf_op jit(solution)/shard_map/all_to_all | solution.py:96
  60.0 5.3 %all-to-all-start.3 = ((bf16[128,8,512]{0,2,1:T(8,128)(2,1)}), bf16[128,8,512]{0,2,1:T(8,128)(2,1)S(1)}, u32[]{:S(2)}, u32[]{:S(2)}) async-start(bf16[128,8,512]{0,2,1:T(8,128)(2,1)} %bitcast.125), calls=%async_computation.3 | async-start | bytes 2097152 | tf_op jit(solution)/shard_map/all_to_all | solution.py:97
  66.6 3.9 %fusion.45 = (f32[8,4,128]{2,0,1:T(8,128)S(1)}, f32[8,4,128,512]{2,3,0,1:T(8,128)S(1)}) fusion(f32[4,512,8,128]{3,1,2,0:T(8,128)S(1)} %fusion.26, pred[512]{0:T(512)(128)(4,1)S(1)} %iota_compare_fusion), kind=kOutput, calls=%fused_computation.75 | output fusion | flops 12583423 | bytes 16794112 | tf_op jit(solution)/shard_map/sub | solution.py:43
  70.5 3.2 %copy-done.1 = f32[8,4,128,512]{2,3,0,1:T(8,128)} copy-done((f32[8,4,128,512]{2,3,0,1:T(8,128)}, f32[8,4,128,512]{2,3,0,1:T(8,128)S(1)}, u32[]{:S(2)}) %copy-start.1) | copy-done | bytes 8388632
  73.7 3.0 %fusion.44 = bf16[8,4,128,512]{2,3,0,1:T(8,128)(2,1)} fusion(f32[8,4,128,512]{2,3,0,1:T(8,128)S(1)} %get-tuple-element.32, f32[8,4,128]{2,0,1:T(8,128)S(1)} %get-tuple-element.31), kind=kLoop, calls=%fused_computation.74 | loop fusion | flops 4194304 | bytes 12599296 | tf_op jit(solution)/shard_map/convert_element_type | solution.py:45
  76.7 13.2 %all-to-all-done.3 = bf16[128,8,512]{0,2,1:T(8,128)(2,1)S(1)} async-done(((bf16[128,8,512]{0,2,1:T(8,128)(2,1)}), bf16[128,8,512]{0,2,1:T(8,128)(2,1)S(1)}, u32[]{:S(2)}, u32[]{:S(2)}) %all-to-all-start.3) | async-done | bytes 1048608 | tf_op jit(solution)/shard_map/all_to_all | solution.py:97
  90.1 4.4 %fusion.24 = (f32[4]{0:T(128)S(1)}, bf16[8,128,4,128]{1,3,0,2:T(8,128)(2,1)S(1)}, bf16[8,128,4,128]{1,3,0,2:T(8,128)(2,1)}) fusion(f32[8,128,4,128]{1,3,2,0:T(8,128)S(1)} %bitcast.121, f32[8,128]{1,0:T(8,128)S(1)} %fusion.40, f32[4]{0:T(128)S(1)} %dynamic_slice.5, bf16[8,4,128,512]{2,3,0,1:T(8,128)(2,1)} %fusion.44, bf16[512,4,128,1]{2,1,0,3:T(4,128)(2,1)S(1)} %bitcast.128), kind=kOutput, calls=%fused_computation.29 | convolution fusion | flops 541589504 | bytes 8917024 | tf_op jit(solution)/shard_map/bhtj,jhd->bthd/dot_general | solution.py:46
  94.5 3.2 %convert_bitcast_fusion = bf16[8,512,4,128]{1,3,2,0:T(8,128)(2,1)} fusion(bf16[8,4,128,512]{2,3,0,1:T(8,128)(2,1)S(1)} %copy-done, bf16[8,128,4,128]{1,3,0,2:T(8,128)(2,1)S(1)} %get-tuple-element.21), kind=kOutput, calls=%fused_computation.17 | convolution fusion | flops 538968064 | bytes 9437184 | tf_op jit(solution)/shard_map/bhtj,bthd->bjhd/dot_general | solution.py:71
  97.7 3.8 %reduce_sum.54 = bf16[512,4,128]{0,2,1:T(8,128)(2,1)} reduce(bf16[8,512,4,128]{1,3,2,0:T(8,128)(2,1)} %convert_bitcast_fusion, bf16[]{:T(256)} %constant.43.clone.1), dimensions={0}, to_apply=%region_4.5 | reduce | flops 1835008 | bytes 4718594 | tf_op jit(solution)/shard_map/reduce_sum | solution.py:77
  105.6 4.4 %all-to-all-start.6 = ((bf16[8,64,512]{2,1,0:T(8,128)(2,1)}), bf16[8,64,512]{2,1,0:T(8,128)(2,1)}, u32[]{:S(2)}, u32[]{:S(2)}) async-start(bf16[8,64,512]{2,1,0:T(8,128)(2,1)} %convert_element_type.73), calls=%async_computation.6 | async-start | bytes 1048576 | tf_op jit(solution)/shard_map/all_to_all | solution.py:124
  109.9 9.9 %fusion.4 = bf16[8,4,128,512]{2,3,0,1:T(8,128)(2,1)} fusion(bf16[8,128,4,128]{1,3,0,2:T(8,128)(2,1)S(1)} %get-tuple-element.21, bf16[512,4,128,1]{2,1,0,3:T(4,128)(2,1)S(1)} %bitcast.129, f32[8,4,128,512]{2,3,0,1:T(8,128)} %copy-done.1, f32[8,4,128]{2,0,1:T(8,128)S(1)} %get-tuple-element.31), kind=kOutput, calls=%fused_computation.7 | convolution fusion | flops 1088426496 | bytes 14172160 | tf_op jit(solution)/shard_map/sub | solution.py:63
  119.9 5.4 %convert_bitcast_fusion.1 = bf16[8,512,4,128]{3,1,2,0:T(8,128)(2,1)} fusion(bf16[8,128,4,128]{1,3,2,0:T(8,128)(2,1)S(1)} %bitcast.123, bf16[8,4,128,512]{2,3,0,1:T(8,128)(2,1)} %fusion.4), kind=kOutput, calls=%fused_computation.18 | convolution fusion | flops 538968064 | bytes 9437184 | tf_op jit(solution)/shard_map/bhtj,bthd->bjhd/dot_general | solution.py:68
  129.5 5.7 %all-to-all-start.5 = ((bf16[8,64,512]{2,1,0:T(8,128)(2,1)}), bf16[8,64,512]{2,1,0:T(8,128)(2,1)S(1)}, u32[]{:S(2)}, u32[]{:S(2)}) async-start(bf16[8,64,512]{2,1,0:T(8,128)(2,1)} %convert_element_type.70), calls=%async_computation.5 | async-start | bytes 1048576 | tf_op jit(solution)/shard_map/all_to_all | solution.py:121
  139.2 9.4 %all-to-all-done.5 = bf16[8,64,512]{2,1,0:T(8,128)(2,1)S(1)} async-done(((bf16[8,64,512]{2,1,0:T(8,128)(2,1)}), bf16[8,64,512]{2,1,0:T(8,128)(2,1)S(1)}, u32[]{:S(2)}, u32[]{:S(2)}) %all-to-all-start.5) | async-done | bytes 524320 | tf_op jit(solution)/shard_map/all_to_all | solution.py:121
  148.6 3.7 %all-to-all-start.4 = ((bf16[8,128,512]{1,2,0:T(8,128)(2,1)}), bf16[8,128,512]{1,2,0:T(8,128)(2,1)S(1)}, u32[]{:S(2)}, u32[]{:S(2)}) async-start(bf16[8,128,512]{1,2,0:T(8,128)(2,1)} %bitcast.28), calls=%async_computation.4 | async-start | bytes 2097152 | tf_op jit(solution)/shard_map/all_to_all | solution.py:118
  153.4 24.2 %all-to-all-done.4 = bf16[8,128,512]{1,2,0:T(8,128)(2,1)S(1)} async-done(((bf16[8,128,512]{1,2,0:T(8,128)(2,1)}), bf16[8,128,512]{1,2,0:T(8,128)(2,1)S(1)}, u32[]{:S(2)}, u32[]{:S(2)}) %all-to-all-start.4) | async-done | bytes 1048608 | tf_op jit(solution)/shard_map/all_to_all | solution.py:118
  177.6 3.6 %all-to-all-start.2 = ((bf16[8,128,512]{1,2,0:T(8,128)(2,1)}), bf16[8,128,512]{1,2,0:T(8,128)(2,1)S(1)}, u32[]{:S(2)}, u32[]{:S(2)}) async-start(bf16[8,128,512]{1,2,0:T(8,128)(2,1)} %bitcast.18), calls=%async_computation.2 | async-start | bytes 2097152 | tf_op jit(solution)/shard_map/all_to_all | solution.py:117
  181.4 45.7 %psum.7 = f32[32]{0:T(128)} all-reduce(f32[32]{0:T(128)S(1)} %dynamic_update_slice.3), channel_id=1, replica_groups=mesh['seq'=8,'dp'=4,'grp'=1] {'seq','dp','grp'}, use_global_device_ids=true, to_apply=%region_6.7 | all-reduce | flops 32 | bytes 256 | tf_op jit(solution)/shard_map/psum | solution.py:132
  (71 shorter events, 45.7 us)
Async XLA Ops:
  0.6 33.1 %copy-start.3 = (bf16[1,128,4096]{2,1,0:T(8,128)(2,1)S(1)}, bf16[1,128,4096]{2,1,0:T(8,128)(2,1)}, u32[]{:S(2)}) copy-start(bf16[1,128,4096]{2,1,0:T(8,128)(2,1)} %param.10) | copy-start | bytes 3145732
  0.6 34.5 %copy-start.4 = (f32[32]{0:T(128)S(1)}, f32[32]{0:T(128)}, u32[]{:S(2)}) copy-start(f32[32]{0:T(128)} %param.11) | copy-start | bytes 388
  2.9 26.0 %all-to-all-start = ((bf16[64,8,512]{2,0,1:T(8,128)(2,1)}), bf16[64,8,512]{2,0,1:T(8,128)(2,1)S(1)}, u32[]{:S(2)}, u32[]{:S(2)}) async-start(bf16[64,8,512]{2,0,1:T(8,128)(2,1)} %copy.65), calls=%async_computation | async-start | bytes 1048576 | tf_op jit(solution)/shard_map/all_to_all | solution.py:100
  13.3 21.9 %collective-permute-start = (bf16[64,512]{1,0:T(8,128)(2,1)}, bf16[64,512]{1,0:T(8,128)(2,1)}, u32[]{:S(2)}, u32[]{:S(2)}) collective-permute-start(bf16[64,512]{1,0:T(8,128)(2,1)} %bitcast.118), channel_id=1, source_target_pairs={{0,4},{4,0},{8,12},{12,8},{16,20},{20,16},{24,28},{28,24},{1,5},{5... | collective-permute-start | bytes 196616 | tf_op jit(solution)/shard_map/ppermute | solution.py:24
  16.0 23.9 %collective-permute-start.1 = (bf16[64,512]{1,0:T(8,128)(2,1)}, bf16[64,512]{1,0:T(8,128)(2,1)}, u32[]{:S(2)}, u32[]{:S(2)}) collective-permute-start(bf16[64,512]{1,0:T(8,128)(2,1)} %bitcast.117), channel_id=1, source_target_pairs={{0,8},{4,12},{8,0},{12,4},{16,24},{20,28},{24,16},{28,20},{1,9},{5... | collective-permute-start | bytes 196616 | tf_op jit(solution)/shard_map/ppermute | solution.py:24
  18.1 24.1 %collective-permute-start.2 = (bf16[64,512]{1,0:T(8,128)(2,1)}, bf16[64,512]{1,0:T(8,128)(2,1)}, u32[]{:S(2)}, u32[]{:S(2)}) collective-permute-start(bf16[64,512]{1,0:T(8,128)(2,1)} %bitcast.116), channel_id=1, source_target_pairs={{0,12},{4,8},{8,4},{12,0},{16,28},{20,24},{24,20},{28,16},{1,13},{... | collective-permute-start | bytes 196616 | tf_op jit(solution)/shard_map/ppermute | solution.py:24
  18.1 24.9 %collective-permute-start.3 = (bf16[64,512]{1,0:T(8,128)(2,1)S(1)}, bf16[64,512]{1,0:T(8,128)(2,1)}, u32[]{:S(2)}, u32[]{:S(2)}) collective-permute-start(bf16[64,512]{1,0:T(8,128)(2,1)S(1)} %bitcast.137), channel_id=1, source_target_pairs={{0,16},{4,20},{8,24},{12,28},{16,0},{20,4},{24,8},{28,12},{1,17},{... | collective-permute-start | bytes 196616 | tf_op jit(solution)/shard_map/ppermute | solution.py:24
  21.1 22.7 %collective-permute-start.4 = (bf16[64,512]{1,0:T(8,128)(2,1)S(1)}, bf16[64,512]{1,0:T(8,128)(2,1)}, u32[]{:S(2)}, u32[]{:S(2)}) collective-permute-start(bf16[64,512]{1,0:T(8,128)(2,1)S(1)} %bitcast.136), channel_id=1, source_target_pairs={{0,20},{4,16},{8,28},{12,24},{16,4},{20,0},{24,12},{28,8},{1,21},{... | collective-permute-start | bytes 196616 | tf_op jit(solution)/shard_map/ppermute | solution.py:24
  28.9 31.1 %all-to-all-start.1 = ((bf16[128,8,512]{0,2,1:T(8,128)(2,1)}), bf16[128,8,512]{0,2,1:T(8,128)(2,1)S(1)}, u32[]{:S(2)}, u32[]{:S(2)}) async-start(bf16[128,8,512]{0,2,1:T(8,128)(2,1)} %bitcast.12), calls=%async_computation.1 | async-start | bytes 2097152 | tf_op jit(solution)/shard_map/all_to_all | solution.py:96
  35.2 18.0 %collective-permute-start.5 = (bf16[64,512]{1,0:T(8,128)(2,1)}, bf16[64,512]{1,0:T(8,128)(2,1)S(1)}, u32[]{:S(2)}, u32[]{:S(2)}) collective-permute-start(bf16[64,512]{1,0:T(8,128)(2,1)} %bitcast.139), channel_id=1, source_target_pairs={{0,24},{4,28},{8,16},{12,20},{16,8},{20,12},{24,0},{28,4},{1,25},{... | collective-permute-start | bytes 196616 | tf_op jit(solution)/shard_map/ppermute | solution.py:24
  39.8 14.8 %collective-permute-start.6 = (bf16[64,512]{1,0:T(8,128)(2,1)S(1)}, bf16[64,512]{1,0:T(8,128)(2,1)S(1)}, u32[]{:S(2)}, u32[]{:S(2)}) collective-permute-start(bf16[64,512]{1,0:T(8,128)(2,1)S(1)} %bitcast.138), channel_id=1, source_target_pairs={{0,28},{4,24},{8,20},{12,16},{16,12},{20,8},{24,4},{28,0},{1,29},{... | collective-permute-start | bytes 196616 | tf_op jit(solution)/shard_map/ppermute | solution.py:24
  60.0 30.0 %all-to-all-start.3 = ((bf16[128,8,512]{0,2,1:T(8,128)(2,1)}), bf16[128,8,512]{0,2,1:T(8,128)(2,1)S(1)}, u32[]{:S(2)}, u32[]{:S(2)}) async-start(bf16[128,8,512]{0,2,1:T(8,128)(2,1)} %bitcast.125), calls=%async_computation.3 | async-start | bytes 2097152 | tf_op jit(solution)/shard_map/all_to_all | solution.py:97
  70.5 3.2 %copy-start.1 = (f32[8,4,128,512]{2,3,0,1:T(8,128)}, f32[8,4,128,512]{2,3,0,1:T(8,128)S(1)}, u32[]{:S(2)}) copy-start(f32[8,4,128,512]{2,3,0,1:T(8,128)S(1)} %get-tuple-element.32) | copy-start | bytes 25165828
  89.9 4.6 %copy-start = (bf16[8,4,128,512]{2,3,0,1:T(8,128)(2,1)S(1)}, bf16[8,4,128,512]{2,3,0,1:T(8,128)(2,1)}, u32[]{:S(2)}) copy-start(bf16[8,4,128,512]{2,3,0,1:T(8,128)(2,1)} %fusion.44) | copy-start | bytes 12582916
  105.6 23.9 %all-to-all-start.6 = ((bf16[8,64,512]{2,1,0:T(8,128)(2,1)}), bf16[8,64,512]{2,1,0:T(8,128)(2,1)}, u32[]{:S(2)}, u32[]{:S(2)}) async-start(bf16[8,64,512]{2,1,0:T(8,128)(2,1)} %convert_element_type.73), calls=%async_computation.6 | async-start | bytes 1048576 | tf_op jit(solution)/shard_map/all_to_all | solution.py:124
  128.1 24.2 %copy-start.2 = (bf16[8,128,4,128]{1,3,0,2:T(8,128)(2,1)S(1)}, bf16[8,128,4,128]{1,3,0,2:T(8,128)(2,1)}, u32[]{:S(2)}) copy-start(bf16[8,128,4,128]{1,3,0,2:T(8,128)(2,1)} %get-tuple-element.22) | copy-start | bytes 3145732
  129.5 19.1 %all-to-all-start.5 = ((bf16[8,64,512]{2,1,0:T(8,128)(2,1)}), bf16[8,64,512]{2,1,0:T(8,128)(2,1)S(1)}, u32[]{:S(2)}, u32[]{:S(2)}) async-start(bf16[8,64,512]{2,1,0:T(8,128)(2,1)} %convert_element_type.70), calls=%async_computation.5 | async-start | bytes 1048576 | tf_op jit(solution)/shard_map/all_to_all | solution.py:121
  148.6 28.9 %all-to-all-start.4 = ((bf16[8,128,512]{1,2,0:T(8,128)(2,1)}), bf16[8,128,512]{1,2,0:T(8,128)(2,1)S(1)}, u32[]{:S(2)}, u32[]{:S(2)}) async-start(bf16[8,128,512]{1,2,0:T(8,128)(2,1)} %bitcast.28), calls=%async_computation.4 | async-start | bytes 2097152 | tf_op jit(solution)/shard_map/all_to_all | solution.py:118
  177.6 54.6 %all-to-all-start.2 = ((bf16[8,128,512]{1,2,0:T(8,128)(2,1)}), bf16[8,128,512]{1,2,0:T(8,128)(2,1)S(1)}, u32[]{:S(2)}, u32[]{:S(2)}) async-start(bf16[8,128,512]{1,2,0:T(8,128)(2,1)} %bitcast.18), calls=%async_computation.2 | async-start | bytes 2097152 | tf_op jit(solution)/shard_map/all_to_all | solution.py:117
